TPU v7x, 32 devices: a whole 2x2x4 slice. The times are simulated.
32 devices in a mesh: row: 4 (over x, core), col: 8 (over z, y).
Axes of the slice: x: 2, y: 2, z: 4, core: 2. Of those that a mesh axis runs over, the one named last changes fastest.
Arguments:
- features: bfloat16 [4096, 256], P(('row', 'col')), may hold values from -192 to 192
- grad_out: bfloat16 [4096, 256], P(('row', 'col')), may hold values from -192 to 192
- tile_weight: bfloat16 [2048, 128, 128], P(('row', 'col')), may hold values from 0 to 256, as said below
- tile_list: int32 [128, 3, 32], P(('row', 'col')), may hold values from -1 to 63, as said below
Outputs:
- aggregated: bfloat16 [4096, 256], P(('row', 'col'))
- feature_grad: bfloat16 [4096, 256], P(('row', 'col'))
Inputs may be any that keep to these rules, and one draw needn't show every extreme that they name: `tile_list`: each column of a list is a slot (tile number, source block below 1, destination block below 8); tile number -1 marks an empty slot, whose blocks are 0. The tile numbers listed by one device are distinct and are 0 to n - 1 for some n between 40 and 64; some device lists all 64. On every device some step has all 32 slots used. Stored tiles that no slot lists take no part. `tile_weight`: entries are whole numbers.
All inputs are finite; a program needn't handle non-finite values.
Results may differ from a plain program's by a relative error of at most 0.017.
Values may be sent and summed in bfloat16 or wider, within the bound.
No kernel may reach another device: no remote copies, remote signals or barrier semaphores. Data moves between devices by JAX's collectives and lax.ppermute only.
A program may use at most 64 MiB of HBM per device.

v0:
```python
import math
import jax
import jax.numpy as jnp
from jax import lax
from jax.sharding import PartitionSpec as P


def passed_along(value, axis, steps):
    count = lax.axis_size(axis)
    pairs = [(source, (source + steps) % count) for source in range(count)]
    return lax.ppermute(value, axis, pairs)


def local(features, grad_out, tile_weight, tile_list):
    step_count = lax.axis_size("row")
    columns = lax.axis_size("col")
    row_pos = lax.axis_index("row")
    slot_count = tile_list.shape[2]
    tiles_here = tile_weight.shape[0]
    tile_len = tile_weight.shape[1]
    feat_width = features.shape[1]
    src_blocks = features.shape[0] // tile_len
    dst_blocks = columns * (grad_out.shape[0] // tile_len)
    flat_ids = tile_list[:, 0, :].reshape(-1)
    flat_step = jnp.arange(step_count * slot_count, dtype=jnp.int32) // slot_count
    matches = (flat_ids[None, :] == jnp.arange(tiles_here, dtype=jnp.int32)[:, None]).astype(
        jnp.int32
    )
    tile_used = jnp.sum(matches, axis=1)
    tile_step = jnp.sum(matches * flat_step[None, :], axis=1)
    tile_src = jnp.sum(matches * tile_list[:, 1, :].reshape(-1)[None, :], axis=1)
    tile_dst = jnp.sum(matches * tile_list[:, 2, :].reshape(-1)[None, :], axis=1)
    owner_row = (row_pos - tile_step) % step_count
    src_slot = owner_row * src_blocks + tile_src
    used_float = tile_used.astype(jnp.float32)
    row_sums = jnp.sum(tile_weight, axis=2, dtype=jnp.float32)
    col_sums = jnp.sum(tile_weight, axis=1, dtype=jnp.float32)
    dst_pick = (tile_dst[:, None] == jnp.arange(dst_blocks, dtype=jnp.int32)[None, :]).astype(
        jnp.float32
    ) * used_float[:, None]
    src_pick = (
        src_slot[:, None] == jnp.arange(step_count * src_blocks, dtype=jnp.int32)[None, :]
    ).astype(jnp.float32) * used_float[:, None]
    dst_terms = jnp.dot(dst_pick.T, row_sums, precision=lax.Precision.HIGHEST).reshape(-1)
    src_terms = jnp.dot(src_pick.T, col_sums, precision=lax.Precision.HIGHEST).reshape(-1)
    src_scale = lax.rsqrt(1.0 + lax.psum_scatter(src_terms, "row", scatter_dimension=0, tiled=True))
    dst_scale = lax.rsqrt(1.0 + lax.psum_scatter(dst_terms, "col", scatter_dimension=0, tiled=True))
    scaled = (features.astype(jnp.float32) * src_scale[:, None]).astype(jnp.bfloat16)
    scaled = scaled.reshape(src_blocks, tile_len, feat_width)
    scaled_grads = (grad_out.astype(jnp.float32) * dst_scale[:, None]).astype(jnp.bfloat16)
    grad_rows = lax.all_gather(scaled_grads, "col", axis=0, tiled=True).reshape(
        dst_blocks, tile_len, feat_width
    )

    def pick_tiles(list_step):
        tile_ids = tile_list[list_step, 0]
        keep_mask = (tile_ids >= 0).astype(jnp.bfloat16)
        chosen = tile_weight[jnp.maximum(tile_ids, 0)] * keep_mask[:, None, None]
        return (chosen, tile_list[list_step, 1], tile_list[list_step, 2])

    def backward_add(accum_total, rows, list_step):
        chosen, src_index, dst_index = pick_tiles(list_step)
        products = jnp.einsum(
            "kij,kif->kjf", chosen, rows[dst_index], preferred_element_type=jnp.float32
        )
        return accum_total.at[src_index].add(products)

    def grad_step(grad_state, step_pos):
        return backward_add(grad_state, grad_rows, step_count - 1 - step_pos)

    def grad_move(grad_state):
        return passed_along(grad_state.astype(jnp.bfloat16), "row", -1).astype(grad_state.dtype)

    partial_zero = jnp.zeros((dst_blocks, tile_len, feat_width), jnp.float32)
    everything = lax.all_gather(scaled, "row", axis=0, tiled=True)
    batch_size = math.gcd(tiles_here, 16)

    def tile_batch(loop_index, partial_value):
        first_tile = loop_index * batch_size
        tile_block = lax.dynamic_slice_in_dim(tile_weight, first_tile, batch_size, 0)
        keep_mask = lax.dynamic_slice_in_dim(tile_used, first_tile, batch_size, 0).astype(
            jnp.bfloat16
        )
        src_index = lax.dynamic_slice_in_dim(src_slot, first_tile, batch_size, 0)
        dst_index = lax.dynamic_slice_in_dim(tile_dst, first_tile, batch_size, 0)
        chosen = tile_block * keep_mask[:, None, None]
        products = jnp.einsum(
            "kij,kjf->kif", chosen, everything[src_index], preferred_element_type=jnp.float32
        )
        return partial_value.at[dst_index].add(products)

    partial_value = lax.fori_loop(0, tiles_here // batch_size, tile_batch, partial_zero)

    def grad_loop(step_pos, grad_state):
        return grad_move(grad_step(grad_state, step_pos))

    grad_state = lax.fori_loop(
        0, step_count - 1, grad_loop, jnp.zeros((src_blocks, tile_len, feat_width), jnp.float32)
    )
    grad_state = grad_step(grad_state, step_count - 1)
    summed = lax.psum_scatter(
        partial_value.reshape(dst_blocks * tile_len, feat_width).astype(jnp.bfloat16),
        "col",
        scatter_dimension=0,
        tiled=True,
    ).astype(jnp.float32)
    aggregated = (summed * dst_scale[:, None]).astype(jnp.bfloat16)
    grads = grad_state.reshape(src_blocks * tile_len, feat_width)
    feature_grad = (grads * src_scale[:, None]).astype(jnp.bfloat16)
    return (aggregated, feature_grad)


def solution(mesh):
    return jax.shard_map(
        local,
        mesh=mesh,
        in_specs=(
            P(("row", "col"), None),
            P(("row", "col"), None),
            P(("row", "col"), None, None),
            P(("row", "col"), None, None),
        ),
        out_specs=(P(("row", "col"), None), P(("row", "col"), None)),
        check_vma=False,
    )
```

profile of v0, /device:TPU:0, one launch (start us, length us, event | category | flops | bytes accessed | tf_op | source)
XLA Modules:
  0.0 244.0 jit_solution(11328118093270040016)
XLA Ops:
  15.8 2.3 convert_reduce_fusion
  18.3 8.4 %all-reduce = f32[512]{0:T(512)S(1)} all-reduce(f32[512]{0:T(512)S(1)} %convolution_bitcast_fusion.1), channel_id=3, replica_groups=mesh['row'=4,'col'=8] {'row'}, use_global_device_ids=true, to_apply=%region_5.6.clone | all-reduce | flops 512 | bytes 4096
  26.9 21.7 %all-reduce.1 = f32[1024]{0:T(1024)S(1)} all-reduce(f32[1024]{0:T(1024)S(1)} %convolution_bitcast_fusion), channel_id=5, replica_groups=mesh['row'=4,'col'=8] {'col'}, use_global_device_ids=true, to_apply=%region_11.12.clone | all-reduce | flops 1024 | bytes 8192
  48.8 31.5 %all_gather.7 = bf16[1024,256]{1,0:T(8,128)(2,1)S(1)} all-gather(bf16[128,256]{1,0:T(8,128)(2,1)S(1)} %multiply_convert_fusion), channel_id=1, replica_groups=mesh['row'=4,'col'=8] {'col'}, dimensions={0}, use_global_device_ids=true | all-gather | bytes 589824 | tf_op jit(solution)/shard_map/all_gather | solution.py:51
  82.1 2.0 gather_fusion.4
  84.1 5.0 %fusion.13 = f32[32,128,256]{2,1,0:T(8,128)} fusion(bf16[32,128,256]{2,1,0:T(8,128)(2,1)} %gather_fusion.4, bf16[32,128,128]{2,1,0:T(8,128)(2,1)} %gather_fusion.3, bf16[32]{0:T(256)(128)(2,1)S(1)} %fusion.26), kind=kOutput, calls=%fused_computation.41 | convolution fusion | flops 268959744 | bytes 7340096 | tf_op jit(solution)/shard_map/kij,kif->kjf/dot_general | solution.py:63
  89.0 49.5 %while.30 = (s32[]{:T(128)}, f32[1,128,256]{2,1,0:T(8,128)S(1)}, s32[4,3,32]{2,1,0:T(4,128)S(1)}, bf16[64,128,128]{2,1,0:T(8,128)(2,1)S(1)}, bf16[8,128,256]{2,1...) while((s32[]{:T(128)}, f32[1,128,256]{2,1,0:T(8,128)S(1)}, ...), condition=%wide.region_14.15_spmd.clone, body=%wide.region_12.14_spmd.clone.sunk | while | flops 270109056 | bytes 35530608 | solution.py:97
  89.1 1.7 gather_fusion.2
  91.6 4.3 %fusion.57 = f32[32,128,256]{2,1,0:T(8,128)} fusion(bf16[32,128,256]{2,1,0:T(8,128)(2,1)S(1)} %gather_fusion.1, bf16[32,128,128]{2,1,0:T(8,128)(2,1)} %gather_fusion.2, bf16[32]{0:T(256)(128)(2,1)S(1)} %fusion.56), kind=kOutput, calls=%fused_computation.17.clone.1 | convolution fusion | flops 268959744 | bytes 7340096 | tf_op jit(solution)/shard_map/while/body/eval_jaxpr/kij,kif->kjf/dot_general | solution.py:63
  95.9 6.4 %scatter_fusion.1 = f32[128,256,1]{1,0,2:T(8,128)S(1)} fusion(f32[128,256,1]{1,0,2:T(8,128)S(1)} %select_bitcast_fusion.2, s32[32]{0:T(128)S(1)} %fusion.54, f32[32,128,256]{2,1,0:T(8,128)} %fusion.57), kind=kCustom, calls=%fused_computation.6.clone.clone.1 | custom fusion | flops 1048576 | bytes 12583040 | tf_op jit(solution)/shard_map/while/body/eval_jaxpr/scatter-add | solution.py:66
  102.4 1.9 collective-permute-done
  104.5 1.7 gather_fusion.2
  106.9 4.3 %fusion.57 = f32[32,128,256]{2,1,0:T(8,128)} fusion(bf16[32,128,256]{2,1,0:T(8,128)(2,1)S(1)} %gather_fusion.1, bf16[32,128,128]{2,1,0:T(8,128)(2,1)} %gather_fusion.2, bf16[32]{0:T(256)(128)(2,1)S(1)} %fusion.56), kind=kOutput, calls=%fused_computation.17.clone.1 | convolution fusion | flops 268959744 | bytes 7340096 | tf_op jit(solution)/shard_map/while/body/eval_jaxpr/kij,kif->kjf/dot_general | solution.py:63
  111.2 6.4 %scatter_fusion.1 = f32[128,256,1]{1,0,2:T(8,128)S(1)} fusion(f32[128,256,1]{1,0,2:T(8,128)S(1)} %select_bitcast_fusion.2, s32[32]{0:T(128)S(1)} %fusion.54, f32[32,128,256]{2,1,0:T(8,128)} %fusion.57), kind=kCustom, calls=%fused_computation.6.clone.clone.1 | custom fusion | flops 1048576 | bytes 12583040 | tf_op jit(solution)/shard_map/while/body/eval_jaxpr/scatter-add | solution.py:66
  117.7 1.8 collective-permute-start
  119.5 1.9 collective-permute-done
  124.0 4.3 %fusion.57 = f32[32,128,256]{2,1,0:T(8,128)} fusion(bf16[32,128,256]{2,1,0:T(8,128)(2,1)S(1)} %gather_fusion.1, bf16[32,128,128]{2,1,0:T(8,128)(2,1)} %gather_fusion.2, bf16[32]{0:T(256)(128)(2,1)S(1)} %fusion.56), kind=kOutput, calls=%fused_computation.17.clone.1 | convolution fusion | flops 268959744 | bytes 7340096 | tf_op jit(solution)/shard_map/while/body/eval_jaxpr/kij,kif->kjf/dot_general | solution.py:63
  128.3 6.4 %scatter_fusion.1 = f32[128,256,1]{1,0,2:T(8,128)S(1)} fusion(f32[128,256,1]{1,0,2:T(8,128)S(1)} %select_bitcast_fusion.2, s32[32]{0:T(128)S(1)} %fusion.54, f32[32,128,256]{2,1,0:T(8,128)} %fusion.57), kind=kCustom, calls=%fused_computation.6.clone.clone.1 | custom fusion | flops 1048576 | bytes 12583040 | tf_op jit(solution)/shard_map/while/body/eval_jaxpr/scatter-add | solution.py:66
  134.8 1.8 collective-permute-start
  136.6 1.9 collective-permute-done
  138.6 6.3 %scatter_fusion.2 = f32[128,256,1]{1,0,2:T(8,128)S(1)} fusion(f32[128,256,1]{1,0,2:T(8,128)S(1)} %bitcast.83, s32[32]{0:T(128)S(1)} %fusion.27, f32[32,128,256]{2,1,0:T(8,128)} %fusion.13), kind=kCustom, calls=%fused_computation.7 | custom fusion | flops 1048576 | bytes 12583040 | tf_op jit(solution)/shard_map/scatter-add | solution.py:66
  145.6 6.0 %all-gather = bf16[512,256]{1,0:T(8,128)(2,1)S(1)} all-gather(bf16[128,256]{1,0:T(8,128)(2,1)S(1)} %get-tuple-element.329), channel_id=2, replica_groups=mesh['row'=4,'col'=8] {'row'}, dimensions={0}, use_global_device_ids=true | all-gather | bytes 327680 | tf_op jit(solution)/shard_map/all_gather | solution.py:75
  151.7 23.5 %while.29 = (s32[]{:T(128)}, f32[8,128,256]{2,1,0:T(8,128)S(1)}, s32[64]{0:T(128)S(1)}, bf16[64,128,128]{2,1,0:T(8,128)(2,1)}, s32[64]{0:T(128)S(1)}, /*index=5*...) while((s32[]{:T(128)}, f32[8,128,256]{2,1,0:T(8,128)S(1)}, ...), condition=%wide.region_8.9_spmd, body=%wide.region_6.8_spmd.sunk | while | flops 135005296 | bytes 12063463 | solution.py:92
  153.5 1.9 fusion.51
  155.4 2.2 scatter_fusion
  159.3 1.9 fusion.51
  161.2 2.2 scatter_fusion
  165.2 1.9 fusion.51
  167.1 2.2 scatter_fusion
  171.1 1.9 fusion.51
  173.0 2.2 scatter_fusion
  176.0 59.6 %reduce-scatter.2.cloned.1.call-done = bf16[128,256]{1,0:T(8,128)(2,1)} async-done(((bf16[1024,256]{1,0:T(8,128)(2,1)}), bf16[128,256]{1,0:T(8,128)(2,1)}) %reduce-scatter.2.cloned.1.call-update) | async-done | bytes 65552 | tf_op jit(solution)/shard_map/reduce_scatter | solution.py:101
  (90 shorter events, 24.2 us)
Async XLA Ops:
  7.2 73.1 %copy-start = (bf16[64,128,128]{2,1,0:T(8,128)(2,1)S(1)}, bf16[64,128,128]{2,1,0:T(8,128)(2,1)}, u32[]{:S(2)}) copy-start(bf16[64,128,128]{2,1,0:T(8,128)(2,1)} %param.10) | copy-start | bytes 6291460
  7.2 41.5 %copy-start.3 = (bf16[128,256]{1,0:T(8,128)(2,1)S(1)}, bf16[128,256]{1,0:T(8,128)(2,1)}, u32[]{:S(2)}) copy-start(bf16[128,256]{1,0:T(8,128)(2,1)} %param.9) | copy-start | bytes 196612
  7.2 228.4 %reduce-scatter.2.cloned.1.call-start = ((), (), s32[]{:S(2)}) async-start(), calls=%async_computation.1 | async-start | bytes 589824 | tf_op jit(solution)/shard_map/reduce_scatter | solution.py:101
  95.9 8.4 %copy-start.1 = (bf16[64,128,128]{2,1,0:T(8,128)(2,1)S(1)}, bf16[64,128,128]{2,1,0:T(8,128)(2,1)}, u32[]{:S(2)}) copy-start(bf16[64,128,128]{2,1,0:T(8,128)(2,1)} %get-tuple-element.478) | copy-start | bytes 6291460 | tf_op jit(solution)/shard_map/while
  102.3 2.0 collective-permute-start
  111.2 10.2 %copy-start.1 = (bf16[64,128,128]{2,1,0:T(8,128)(2,1)S(1)}, bf16[64,128,128]{2,1,0:T(8,128)(2,1)}, u32[]{:S(2)}) copy-start(bf16[64,128,128]{2,1,0:T(8,128)(2,1)} %get-tuple-element.478) | copy-start | bytes 6291460 | tf_op jit(solution)/shard_map/while
  117.7 3.7 %collective-permute-start = (bf16[1,128,256]{2,1,0:T(8,128)(2,1)S(1)}, bf16[1,128,256]{2,1,0:T(8,128)(2,1)S(1)}, u32[]{:S(2)}, u32[]{:S(2)}) collective-permute-start(bf16[1,128,256]{2,1,0:T(8,128)(2,1)S(1)} %convert_bitcast_fusion.2), channel_id=1, source_target_pairs={{0,24},{8,0},{16,8},{24,16},{1,25},{9,1},{17,9},{25,17},{2,26},{10... | collective-permute-start | bytes 196616 | tf_op jit(solution)/shard_map/while/body/eval_jaxpr/ppermute | solution.py:11
  128.3 10.2 %copy-start.1 = (bf16[64,128,128]{2,1,0:T(8,128)(2,1)S(1)}, bf16[64,128,128]{2,1,0:T(8,128)(2,1)}, u32[]{:S(2)}) copy-start(bf16[64,128,128]{2,1,0:T(8,128)(2,1)} %get-tuple-element.478) | copy-start | bytes 6291460 | tf_op jit(solution)/shard_map/while
  134.8 3.7 %collective-permute-start = (bf16[1,128,256]{2,1,0:T(8,128)(2,1)S(1)}, bf16[1,128,256]{2,1,0:T(8,128)(2,1)S(1)}, u32[]{:S(2)}, u32[]{:S(2)}) collective-permute-start(bf16[1,128,256]{2,1,0:T(8,128)(2,1)S(1)} %convert_bitcast_fusion.2), channel_id=1, source_target_pairs={{0,24},{8,0},{16,8},{24,16},{1,25},{9,1},{17,9},{25,17},{2,26},{10... | collective-permute-start | bytes 196616 | tf_op jit(solution)/shard_map/while/body/eval_jaxpr/ppermute | solution.py:11
  138.6 6.4 %copy-start.2 = (bf16[128,256]{1,0:T(8,128)(2,1)S(1)}, bf16[128,256]{1,0:T(8,128)(2,1)}, u32[]{:S(2)}) copy-start(bf16[128,256]{1,0:T(8,128)(2,1)} %param.8) | copy-start | bytes 196612
Sparse Core Ops, SparseCore 0:
  176.1 59.4 reduce-scatter.1
where the time goes:
time: 245 us; the launch traced here: 244 us
  blocking collectives  67.5 us (28%)
  waiting for transfers between devices  65.3 us (27%)
  other arithmetic  43.9 us (18%)
  matrix products  25.9 us (11%)
  local copies, waits for them, and re-layouts  21.7 us (9%)
  between operations  15.4 us (6%)
  starting transfers between devices  3.77 us (2%)
    reduce_scatter x1, waiting for transfers between devices, local(): lax.psum_scatter(partial_value.reshape(dst_blocks * tile_len, feat_width)...  59.6 us
    all_gather x1, blocking collectives, local(): lax.all_gather(scaled_grads, 'col', axis=0, tiled=True)  31.5 us
    unnamed x2, blocking collectives  30 us
    scatter-add x4, other arithmetic, backward_add(): return accum_total.at[src_index].add(products)  25.6 us
    dot_general x4, matrix products, backward_add(): jnp.einsum('kij,kif->kjf', chosen, rows[dst_index], preferred_element_typ...  17.9 us
    scatter-add x4, other arithmetic, tile_batch(): return partial_value.at[dst_index].add(products)  8.78 us
    dot_general x4, matrix products, tile_batch(): jnp.einsum('kij,kjf->kif', chosen, everything[src_index], preferred_eleme...  7.47 us
    gather x4, local copies, waits for them, and re-layouts, pick_tiles(): chosen = tile_weight[jnp.maximum(tile_ids, 0)] * keep_mask[:, None, None]  6.93 us
  transfers between devices with their start and end apart: 4, of which 4 were waited for; matrix products, arithmetic and copies ran while one was open for 0% of the time, Pallas kernels for 0%

commit v1 on v0

--- a/solution.py
+++ b/solution.py
@@ -1,8 +1,25 @@
+import functools
 import math
 import jax
 import jax.numpy as jnp
 from jax import lax
 from jax.sharding import PartitionSpec as P
+from jax.lax import axis_index, ppermute, psum
+
+
+def pair_trails(page, device_axis, dim_no):
+    oldest, piece_next = (psum(1, device_axis), axis_index(device_axis))
+    k_now, t_next = (page, 1)
+    while t_next < oldest:
+        z_new = ppermute(k_now, device_axis, tuple(((kk, kk ^ t_next) for kk in range(oldest))))
+        e_next = jnp.concatenate([k_now, z_new], dim_no)
+        arr_out = jnp.concatenate([z_new, k_now], dim_no)
+        k_now = jnp.where(piece_next & t_next == 0, e_next, arr_out)
+        t_next = 2 * t_next
+    return k_now
+
+
+words_find = functools.partial(pair_trails, device_axis="col", dim_no=0)
 
 
 def passed_along(value, axis, steps):
@@ -48,9 +65,7 @@
     scaled = (features.astype(jnp.float32) * src_scale[:, None]).astype(jnp.bfloat16)
     scaled = scaled.reshape(src_blocks, tile_len, feat_width)
     scaled_grads = (grad_out.astype(jnp.float32) * dst_scale[:, None]).astype(jnp.bfloat16)
-    grad_rows = lax.all_gather(scaled_grads, "col", axis=0, tiled=True).reshape(
-        dst_blocks, tile_len, feat_width
-    )
+    grad_rows = words_find(scaled_grads).reshape(dst_blocks, tile_len, feat_width)
 
     def pick_tiles(list_step):
         tile_ids = tile_list[list_step, 0]

time: 245 us -> 227 us (0.927)
  blocking collectives: 67.5 us -> 35.4 us
  waiting for transfers between devices: 65.3 us -> 83.4 us
  other arithmetic: 43.9 us -> 41.4 us
    all_gather x1 -> x0, blocking collectives: 31.5 us -> none  [local(): lax.all_gather(scaled_grads, 'col', axis=0, tiled=True)]
    ppermute x0 -> x3, waiting for transfers between devices: none -> 16.4 us  [pair_trails(): ppermute(k_now, device_axis, tuple(((kk, kk ^ t_next) for kk in range(old...]
  transfers between devices with their start and end apart: 4 -> 7, of which waited for: 4 -> 6; matrix products, arithmetic and copies ran while one was open for 0% -> 1% of each run, Pallas kernels for 0% -> 0%
where the time goes in v1:
time: 227 us; the launch traced here: 226 us
  waiting for transfers between devices  83.4 us (37%)
  other arithmetic  41.4 us (18%)
  blocking collectives  35.4 us (16%)
  matrix products  25.9 us (11%)
  local copies, waits for them, and re-layouts  19.8 us (9%)
  between operations  15.6 us (7%)
  starting transfers between devices  3.99 us (2%)
    reduce_scatter x1, waiting for transfers between devices, local(): lax.psum_scatter(partial_value.reshape(dst_blocks * tile_len, feat_width)...  61.3 us
    unnamed x2, blocking collectives  29.1 us
    scatter-add x4, other arithmetic, backward_add(): return accum_total.at[src_index].add(products)  25.6 us
    dot_general x4, matrix products, backward_add(): jnp.einsum('kij,kif->kjf', chosen, rows[dst_index], preferred_element_typ...  17.9 us
    ppermute x3, waiting for transfers between devices, pair_trails(): ppermute(k_now, device_axis, tuple(((kk, kk ^ t_next) for kk in range(old...  16.4 us
    scatter-add x4, other arithmetic, tile_batch(): return partial_value.at[dst_index].add(products)  8.78 us
    dot_general x4, matrix products, tile_batch(): jnp.einsum('kij,kjf->kif', chosen, everything[src_index], preferred_eleme...  7.47 us
    gather x4, local copies, waits for them, and re-layouts, pick_tiles(): chosen = tile_weight[jnp.maximum(tile_ids, 0)] * keep_mask[:, None, None]  6.94 us
  transfers between devices with their start and end apart: 7, of which 6 were waited for; matrix products, arithmetic and copies ran while one was open for 1% of the time, Pallas kernels for 0%

profile of v1, /device:TPU:0, one launch (start us, length us, event | category | flops | bytes accessed | tf_op | source)
XLA Modules:
  0.0 226.0 jit_solution(1540030039732060412)
XLA Ops:
  8.6 2.3 convert_reduce_fusion
  11.1 23.2 %all-reduce.1 = f32[1024]{0:T(1024)S(1)} all-reduce(f32[1024]{0:T(1024)S(1)} %convolution_bitcast_fusion), channel_id=5, replica_groups=mesh['row'=4,'col'=8] {'col'}, use_global_device_ids=true, to_apply=%region_11.12.clone | all-reduce | flops 1024 | bytes 8192
  36.1 3.9 %collective-permute-done.1 = bf16[128,256]{1,0:T(8,128)(2,1)S(1)} collective-permute-done((bf16[128,256]{1,0:T(8,128)(2,1)S(1)}, bf16[128,256]{1,0:T(8,128)(2,1)S(1)}, u32[]{:S(2)}, u32[]{:S(2)}) %collective-permute-start.1) | collective-permute-done | bytes 65568 | tf_op jit(solution)/shard_map/ppermute | solution.py:14
  41.4 6.0 %all-reduce = f32[512]{0:T(512)S(1)} all-reduce(f32[512]{0:T(512)S(1)} %convolution_bitcast_fusion.1), channel_id=3, replica_groups=mesh['row'=4,'col'=8] {'row'}, use_global_device_ids=true, to_apply=%region_5.6.clone | all-reduce | flops 512 | bytes 4096
  49.3 12.5 %collective-permute-done.3 = bf16[512,256]{1,0:T(8,128)(2,1)S(1)} collective-permute-done((bf16[512,256]{1,0:T(8,128)(2,1)S(1)}, bf16[512,256]{1,0:T(8,128)(2,1)S(1)}, u32[]{:S(2)}, u32[]{:S(2)}) %collective-permute-start.3) | collective-permute-done | bytes 262176 | tf_op jit(solution)/shard_map/ppermute | solution.py:14
  62.1 2.0 gather_fusion.4
  64.1 5.0 %fusion.13 = f32[32,128,256]{2,1,0:T(8,128)} fusion(bf16[32,128,256]{2,1,0:T(8,128)(2,1)} %gather_fusion.4, bf16[32,128,128]{2,1,0:T(8,128)(2,1)} %gather_fusion.3, bf16[32]{0:T(256)(128)(2,1)S(1)} %fusion.26), kind=kOutput, calls=%fused_computation.41 | convolution fusion | flops 268959744 | bytes 7340096 | tf_op jit(solution)/shard_map/kij,kif->kjf/dot_general | solution.py:78
  69.0 49.5 %while.30 = (s32[]{:T(128)}, f32[1,128,256]{2,1,0:T(8,128)S(1)}, s32[4,3,32]{2,1,0:T(4,128)S(1)}, bf16[64,128,128]{2,1,0:T(8,128)(2,1)S(1)}, bf16[8,128,256]{2,1...) while((s32[]{:T(128)}, f32[1,128,256]{2,1,0:T(8,128)S(1)}, ...), condition=%wide.region_14.15_spmd.clone, body=%wide.region_12.14_spmd.clone.sunk | while | flops 270109056 | bytes 35530608 | solution.py:112
  69.1 1.7 gather_fusion.2
  71.6 4.3 %fusion.57 = f32[32,128,256]{2,1,0:T(8,128)} fusion(bf16[32,128,256]{2,1,0:T(8,128)(2,1)S(1)} %gather_fusion.1, bf16[32,128,128]{2,1,0:T(8,128)(2,1)} %gather_fusion.2, bf16[32]{0:T(256)(128)(2,1)S(1)} %fusion.56), kind=kOutput, calls=%fused_computation.17.clone.1 | convolution fusion | flops 268959744 | bytes 7340096 | tf_op jit(solution)/shard_map/while/body/eval_jaxpr/kij,kif->kjf/dot_general | solution.py:78
  75.9 6.4 %scatter_fusion.1 = f32[128,256,1]{1,0,2:T(8,128)S(1)} fusion(f32[128,256,1]{1,0,2:T(8,128)S(1)} %select_bitcast_fusion.2, s32[32]{0:T(128)S(1)} %fusion.54, f32[32,128,256]{2,1,0:T(8,128)} %fusion.57), kind=kCustom, calls=%fused_computation.6.clone.clone.1 | custom fusion | flops 1048576 | bytes 12583040 | tf_op jit(solution)/shard_map/while/body/eval_jaxpr/scatter-add | solution.py:81
  82.4 1.9 collective-permute-done
  86.9 4.3 %fusion.57 = f32[32,128,256]{2,1,0:T(8,128)} fusion(bf16[32,128,256]{2,1,0:T(8,128)(2,1)S(1)} %gather_fusion.1, bf16[32,128,128]{2,1,0:T(8,128)(2,1)} %gather_fusion.2, bf16[32]{0:T(256)(128)(2,1)S(1)} %fusion.56), kind=kOutput, calls=%fused_computation.17.clone.1 | convolution fusion | flops 268959744 | bytes 7340096 | tf_op jit(solution)/shard_map/while/body/eval_jaxpr/kij,kif->kjf/dot_general | solution.py:78
  91.2 6.4 %scatter_fusion.1 = f32[128,256,1]{1,0,2:T(8,128)S(1)} fusion(f32[128,256,1]{1,0,2:T(8,128)S(1)} %select_bitcast_fusion.2, s32[32]{0:T(128)S(1)} %fusion.54, f32[32,128,256]{2,1,0:T(8,128)} %fusion.57), kind=kCustom, calls=%fused_computation.6.clone.clone.1 | custom fusion | flops 1048576 | bytes 12583040 | tf_op jit(solution)/shard_map/while/body/eval_jaxpr/scatter-add | solution.py:81
  97.7 1.8 collective-permute-start
  99.5 1.9 collective-permute-done
  104.0 4.3 %fusion.57 = f32[32,128,256]{2,1,0:T(8,128)} fusion(bf16[32,128,256]{2,1,0:T(8,128)(2,1)S(1)} %gather_fusion.1, bf16[32,128,128]{2,1,0:T(8,128)(2,1)} %gather_fusion.2, bf16[32]{0:T(256)(128)(2,1)S(1)} %fusion.56), kind=kOutput, calls=%fused_computation.17.clone.1 | convolution fusion | flops 268959744 | bytes 7340096 | tf_op jit(solution)/shard_map/while/body/eval_jaxpr/kij,kif->kjf/dot_general | solution.py:78
  108.3 6.4 %scatter_fusion.1 = f32[128,256,1]{1,0,2:T(8,128)S(1)} fusion(f32[128,256,1]{1,0,2:T(8,128)S(1)} %select_bitcast_fusion.2, s32[32]{0:T(128)S(1)} %fusion.54, f32[32,128,256]{2,1,0:T(8,128)} %fusion.57), kind=kCustom, calls=%fused_computation.6.clone.clone.1 | custom fusion | flops 1048576 | bytes 12583040 | tf_op jit(solution)/shard_map/while/body/eval_jaxpr/scatter-add | solution.py:81
  114.8 1.8 collective-permute-start
  116.6 1.9 collective-permute-done
  118.6 6.3 %scatter_fusion.2 = f32[128,256,1]{1,0,2:T(8,128)S(1)} fusion(f32[128,256,1]{1,0,2:T(8,128)S(1)} %bitcast.83, s32[32]{0:T(128)S(1)} %fusion.27, f32[32,128,256]{2,1,0:T(8,128)} %fusion.13), kind=kCustom, calls=%fused_computation.7 | custom fusion | flops 1048576 | bytes 12583040 | tf_op jit(solution)/shard_map/scatter-add | solution.py:81
  125.6 6.3 %all-gather = bf16[512,256]{1,0:T(8,128)(2,1)S(1)} all-gather(bf16[128,256]{1,0:T(8,128)(2,1)S(1)} %get-tuple-element.329), channel_id=2, replica_groups=mesh['row'=4,'col'=8] {'row'}, dimensions={0}, use_global_device_ids=true | all-gather | bytes 327680 | tf_op jit(solution)/shard_map/all_gather | solution.py:90
  132.0 23.5 %while.29 = (s32[]{:T(128)}, f32[8,128,256]{2,1,0:T(8,128)S(1)}, s32[64]{0:T(128)S(1)}, bf16[64,128,128]{2,1,0:T(8,128)(2,1)}, s32[64]{0:T(128)S(1)}, /*index=5*...) while((s32[]{:T(128)}, f32[8,128,256]{2,1,0:T(8,128)S(1)}, ...), condition=%wide.region_8.9_spmd, body=%wide.region_6.8_spmd.sunk | while | flops 135005296 | bytes 12063463 | solution.py:107
  133.8 1.9 fusion.51
  135.6 2.2 scatter_fusion
  139.6 1.9 fusion.51
  141.5 2.2 scatter_fusion
  145.5 1.9 fusion.51
  147.4 2.2 scatter_fusion
  151.4 1.9 fusion.51
  153.2 2.2 scatter_fusion
  156.3 61.3 %reduce-scatter.2.cloned.1.call-done = bf16[128,256]{1,0:T(8,128)(2,1)} async-done(((bf16[1024,256]{1,0:T(8,128)(2,1)}), bf16[128,256]{1,0:T(8,128)(2,1)}) %reduce-scatter.2.cloned.1.call-update) | async-done | bytes 65552 | tf_op jit(solution)/shard_map/reduce_scatter | solution.py:116
  (104 shorter events, 21.8 us)
Async XLA Ops:
  7.2 27.1 %copy-start.6 = (u32[32]{0:T(128)S(1)}, u32[32]{0:T(128)}, u32[]{:S(2)}) copy-start(u32[32]{0:T(128)} %constant.179) | copy-start | bytes 388
  7.2 32.9 %copy-start.5 = (u32[32]{0:T(128)S(1)}, u32[32]{0:T(128)}, u32[]{:S(2)}) copy-start(u32[32]{0:T(128)} %constant.175) | copy-start | bytes 388
  7.2 28.6 %copy-start.4 = (s32[4,3,32]{2,0,1:T(4,128)S(1)}, s32[4,3,32]{2,0,1:T(4,128)}, u32[]{:S(2)}) copy-start(s32[4,3,32]{2,0,1:T(4,128)} %param.11) | copy-start | bytes 4612
  7.2 40.4 %copy-start = (bf16[64,128,128]{2,1,0:T(8,128)(2,1)S(1)}, bf16[64,128,128]{2,1,0:T(8,128)(2,1)}, u32[]{:S(2)}) copy-start(bf16[64,128,128]{2,1,0:T(8,128)(2,1)} %param.10) | copy-start | bytes 6291460
  7.2 28.4 %copy-start.3 = (bf16[128,256]{1,0:T(8,128)(2,1)S(1)}, bf16[128,256]{1,0:T(8,128)(2,1)}, u32[]{:S(2)}) copy-start(bf16[128,256]{1,0:T(8,128)(2,1)} %param.9) | copy-start | bytes 196612
  7.2 210.4 %reduce-scatter.2.cloned.1.call-start = ((), (), s32[]{:S(2)}) async-start(), calls=%async_computation.1 | async-start | bytes 589824 | tf_op jit(solution)/shard_map/reduce_scatter | solution.py:116
  35.7 4.3 %collective-permute-start.1 = (bf16[128,256]{1,0:T(8,128)(2,1)S(1)}, bf16[128,256]{1,0:T(8,128)(2,1)S(1)}, u32[]{:S(2)}, u32[]{:S(2)}) collective-permute-start(bf16[128,256]{1,0:T(8,128)(2,1)S(1)} %multiply_convert_fusion), channel_id=1, source_target_pairs={{0,1},{1,0},{2,3},{3,2},{4,5},{5,4},{6,7},{7,6},{8,9},{9,8},{10,11... | collective-permute-start | bytes 196616 | tf_op jit(solution)/shard_map/ppermute | solution.py:14
  40.0 7.3 %collective-permute-start.2 = (bf16[256,256]{1,0:T(8,128)(2,1)S(1)}, bf16[256,256]{1,0:T(8,128)(2,1)S(1)}, u32[]{:S(2)}, u32[]{:S(2)}) collective-permute-start(bf16[256,256]{1,0:T(8,128)(2,1)S(1)} %maximum_select_fusion.2), channel_id=1, source_target_pairs={{0,2},{1,3},{2,0},{3,1},{4,6},{5,7},{6,4},{7,5},{8,10},{9,11},{10,... | collective-permute-start | bytes 393224 | tf_op jit(solution)/shard_map/ppermute | solution.py:14
  47.5 14.4 %collective-permute-start.3 = (bf16[512,256]{1,0:T(8,128)(2,1)S(1)}, bf16[512,256]{1,0:T(8,128)(2,1)S(1)}, u32[]{:S(2)}, u32[]{:S(2)}) collective-permute-start(bf16[512,256]{1,0:T(8,128)(2,1)S(1)} %maximum_select_fusion.1), channel_id=1, source_target_pairs={{0,4},{1,5},{2,6},{3,7},{4,0},{5,1},{6,2},{7,3},{8,12},{9,13},{10,... | collective-permute-start | bytes 786440 | tf_op jit(solution)/shard_map/ppermute | solution.py:14
  75.9 8.4 %copy-start.1 = (bf16[64,128,128]{2,1,0:T(8,128)(2,1)S(1)}, bf16[64,128,128]{2,1,0:T(8,128)(2,1)}, u32[]{:S(2)}) copy-start(bf16[64,128,128]{2,1,0:T(8,128)(2,1)} %get-tuple-element.478) | copy-start | bytes 6291460 | tf_op jit(solution)/shard_map/while
  82.3 2.0 collective-permute-start
  91.2 10.2 %copy-start.1 = (bf16[64,128,128]{2,1,0:T(8,128)(2,1)S(1)}, bf16[64,128,128]{2,1,0:T(8,128)(2,1)}, u32[]{:S(2)}) copy-start(bf16[64,128,128]{2,1,0:T(8,128)(2,1)} %get-tuple-element.478) | copy-start | bytes 6291460 | tf_op jit(solution)/shard_map/while
  97.7 3.7 %collective-permute-start = (bf16[1,128,256]{2,1,0:T(8,128)(2,1)S(1)}, bf16[1,128,256]{2,1,0:T(8,128)(2,1)S(1)}, u32[]{:S(2)}, u32[]{:S(2)}) collective-permute-start(bf16[1,128,256]{2,1,0:T(8,128)(2,1)S(1)} %convert_bitcast_fusion.2), channel_id=1, source_target_pairs={{0,24},{8,0},{16,8},{24,16},{1,25},{9,1},{17,9},{25,17},{2,26},{10... | collective-permute-start | bytes 196616 | tf_op jit(solution)/shard_map/while/body/eval_jaxpr/ppermute | solution.py:28
  108.3 10.2 %copy-start.1 = (bf16[64,128,128]{2,1,0:T(8,128)(2,1)S(1)}, bf16[64,128,128]{2,1,0:T(8,128)(2,1)}, u32[]{:S(2)}) copy-start(bf16[64,128,128]{2,1,0:T(8,128)(2,1)} %get-tuple-element.478) | copy-start | bytes 6291460 | tf_op jit(solution)/shard_map/while
  114.8 3.7 %collective-permute-start = (bf16[1,128,256]{2,1,0:T(8,128)(2,1)S(1)}, bf16[1,128,256]{2,1,0:T(8,128)(2,1)S(1)}, u32[]{:S(2)}, u32[]{:S(2)}) collective-permute-start(bf16[1,128,256]{2,1,0:T(8,128)(2,1)S(1)} %convert_bitcast_fusion.2), channel_id=1, source_target_pairs={{0,24},{8,0},{16,8},{24,16},{1,25},{9,1},{17,9},{25,17},{2,26},{10... | collective-permute-start | bytes 196616 | tf_op jit(solution)/shard_map/while/body/eval_jaxpr/ppermute | solution.py:28
  118.5 6.4 %copy-start.2 = (bf16[128,256]{1,0:T(8,128)(2,1)S(1)}, bf16[128,256]{1,0:T(8,128)(2,1)}, u32[]{:S(2)}) copy-start(bf16[128,256]{1,0:T(8,128)(2,1)} %param.8) | copy-start | bytes 196612
Sparse Core Ops, SparseCore 0:
  156.4 61.1 reduce-scatter.1
